TPU v7x, 256 devices: a whole 4x4x8 slice. The times are simulated.
256 devices in a mesh: row: 16 (over z_hi, y, core), col: 16 (over z_lo, x).
Axes of the slice: x: 4, y: 4, z: 8 (z_hi: 2, z_lo: 4; z = z_hi * 4 + z_lo), core: 2. Of those that a mesh axis runs over, the one named last changes fastest.
Arguments:
- features: bfloat16 [65536, 128], P(('col', 'row')), may hold values from -6 to 6
- weight: bfloat16 [128, 128], replicated, may hold values from -0.5 to 0.5
- tiles: bfloat16 [16, 16, 352, 128, 128], P('row', 'col'), may hold values from -0.0546875 to 0.0546875
- tile_slots: int32 [16, 16, 352], P('row', 'col'), may hold values from 0 to 1023, as said below
- tile_counts: int32 [16, 16], P('row', 'col'), may hold values from 44 to 352, as said below
- cotangent: bfloat16 [65536, 128], P(('row', 'col')), may hold values from -6 to 6
Outputs:
- hidden: bfloat16 [65536, 128], P(('row', 'col'))
- feature_grad: bfloat16 [65536, 128], P(('col', 'row'))
- weight_grad: float32 [128, 128], replicated
Inputs may be any that keep to these rules, and one draw needn't show every extreme that they name: `tile_slots`: the slots of one block are distinct. `tile_counts`: some block has all 352 slots live.
All inputs are finite; a program needn't handle non-finite values.
Results may differ from a plain program's by a relative error of at most 0.006.
Values may be sent and summed in bfloat16 or wider, within the bound.
A program may use at most 128 MiB of HBM per device.

v0:
```python
import math
import jax
import jax.numpy as jnp
from jax import lax
from jax.sharding import PartitionSpec as P


def silu_grad(values):
    sig = jax.nn.sigmoid(values)
    return sig * (1.0 + values * (1.0 - sig))


def body(features, weight, tiles, tile_slots, tile_counts, cotangent):
    tile_vals = tiles[0, 0]
    slot_ids = tile_slots[0, 0]
    live_count = tile_counts[0, 0]
    tile_size = tile_vals.shape[-1]
    share_rows = features.shape[0]
    width = features.shape[1]
    slot_total = slot_ids.shape[0]
    row_count = lax.axis_size("row")
    col_count = lax.axis_size("col")
    tile_rows = share_rows * col_count // tile_size
    tile_cols = share_rows * row_count // tile_size
    col_index = lax.axis_index("col")
    projected = jnp.dot(features, weight, preferred_element_type=jnp.float32).astype(jnp.bfloat16)
    proj_block = lax.all_gather(projected, "row", axis=0, tiled=True)
    is_live = jnp.arange(slot_total, dtype=jnp.int32) < live_count
    gathered = proj_block.reshape(tile_cols, tile_size, width)[slot_ids % tile_cols]
    products = jnp.einsum("tij,tjf->tif", tile_vals, gathered, preferred_element_type=jnp.float32)
    fwd_targets = jnp.where(is_live, slot_ids // tile_cols, tile_rows)
    partial_value = jax.ops.segment_sum(products, fwd_targets, tile_rows + 1)[:tile_rows].reshape(
        tile_rows * tile_size, width
    )
    summed = lax.psum(partial_value, "col")
    own_rows = lax.dynamic_slice_in_dim(summed, col_index * share_rows, share_rows, 0)
    hidden = jax.nn.silu(own_rows).astype(jnp.bfloat16)
    cot_block = lax.all_gather(cotangent, "col", axis=0, tiled=True)
    grad_block = (cot_block.astype(jnp.float32) * silu_grad(summed)).astype(jnp.bfloat16)
    grad_tiles = grad_block.reshape(tile_rows, tile_size, width)[slot_ids // tile_cols]
    back_products = jnp.einsum(
        "tji,tjf->tif", tile_vals, grad_tiles, preferred_element_type=jnp.float32
    )
    back_targets = jnp.where(is_live, slot_ids % tile_cols, tile_cols)
    back_partial = jax.ops.segment_sum(back_products, back_targets, tile_cols + 1)[
        :tile_cols
    ].reshape(tile_cols * tile_size, width)
    grad_proj = lax.psum_scatter(back_partial, "row", scatter_dimension=0, tiled=True).astype(
        jnp.bfloat16
    )
    feature_grad = jnp.dot(grad_proj, weight.T, preferred_element_type=jnp.float32).astype(
        jnp.bfloat16
    )
    weight_term = jnp.dot(features.T, grad_proj, preferred_element_type=jnp.float32)
    node_total = share_rows * row_count * col_count
    weight_grad = lax.psum(weight_term, ("row", "col")) / math.sqrt(node_total)
    return (hidden, feature_grad, weight_grad)


def solution(mesh):
    placed = (
        P(("col", "row"), None),
        P(),
        P("row", "col", None, None, None),
        P("row", "col", None),
        P("row", "col"),
        P(("row", "col"), None),
    )
    return jax.shard_map(
        body,
        mesh=mesh,
        in_specs=placed,
        out_specs=(P(("row", "col"), None), P(("col", "row"), None), P()),
        check_vma=False,
    )
```

profile of v0, /device:TPU:1, one launch (start us, length us, event | category | flops | bytes accessed | tf_op | source)
XLA Modules:
  0.0 771.6 jit_solution(9133756063964806921)
XLA Ops:
  7.2 0.8 copy-done
  8.0 1.5 convolution_convert_fusion.1
  11.0 0.7 fusion.15
  11.7 0.7 fusion.13
  12.4 58.8 %all-gather.3.cloned.1.call-done = bf16[4096,128]{1,0:T(8,128)(2,1)} async-done(((bf16[256,128]{1,0:T(8,128)(2,1)}), bf16[4096,128]{1,0:T(8,128)(2,1)}) %all-gather.3.cloned.1.call-update) | async-done | bytes 1048592 | tf_op jit(solution)/shard_map/all_gather | solution.py:27
  71.3 12.2 %gather_fusion = bf16[352,128,128]{2,1,0:T(8,128)(2,1)} fusion(bf16[32,128,128]{2,1,0:T(8,128)(2,1)} %bitcast.41, s32[1024]{0:T(1024)S(1)} %pad_clamp_fusion.1), kind=kCustom, calls=%fused_computation | custom fusion | bytes 23070080 | tf_op jit(solution)/shard_map/gather | solution.py:29
  83.5 20.6 %fusion.4 = f32[352,128,128]{1,2,0:T(8,128)} fusion(bf16[352,128,128]{2,1,0:T(8,128)(2,1)} %gather_fusion, bf16[1,1,352,128,128]{4,3,2,1,0:T(8,128)(2,1)} %param.8), kind=kOutput, calls=%fused_computation.8 | convolution fusion | flops 1476395008 | bytes 46137344 | tf_op jit(solution)/shard_map/tij,tjf->tif/dot_general | solution.py:30
  104.1 23.5 %copy.13 = f32[352,128,128]{2,1,0:T(8,128)} copy(f32[352,128,128]{1,2,0:T(8,128)} %fusion.4) | data formatting | bytes 46137344 | tf_op jit(solution)/shard_map/tij,tjf->tif/dot_general | solution.py:30
  127.8 46.0 %scatter_fusion = f32[33,128,128]{2,1,0:T(8,128)S(1)} fusion(f32[33,128,128]{2,1,0:T(8,128)S(1)} %broadcast.191.clone, s32[352]{0:T(512)S(1)} %get-tuple-element.10, f32[352,128,128]{2,1,0:T(8,128)} %copy.13), kind=kCustom, calls=%fused_computation.2 | custom fusion | flops 5767168 | bytes 69207424 | tf_op jit(solution)/shard_map/scatter-add | solution.py:32
  173.9 1.5 slice.12
  175.7 153.0 %all-reduce.3.cloned.1.call-done = f32[4096,128]{1,0:T(8,128)} async-done(((f32[4096,128]{1,0:T(8,128)}), f32[4096,128]{1,0:T(8,128)}) %all-reduce.3.cloned.1.call-update) | async-done | bytes 2097168 | tf_op jit(solution)/shard_map/psum | solution.py:35
  328.6 2.6 multiply_convert_fusion
  331.3 11.0 %gather_fusion.1 = bf16[352,128,128]{2,1,0:T(8,128)(2,1)} fusion(bf16[32,128,128]{2,1,0:T(8,128)(2,1)S(1)} %bitcast.40, s32[1024]{0:T(1024)S(1)} %pad_clamp_fusion), kind=kCustom, calls=%fused_computation.1 | custom fusion | bytes 23070080 | tf_op jit(solution)/shard_map/gather | solution.py:40
  342.3 14.4 %fusion.7 = f32[352,128,128]{1,2,0:T(8,128)} fusion(bf16[352,128,128]{2,1,0:T(8,128)(2,1)} %gather_fusion.1, bf16[1,1,352,128,128]{4,3,2,1,0:T(8,128)(2,1)} %param.8), kind=kOutput, calls=%fused_computation.9 | convolution fusion | flops 1476395008 | bytes 46137344 | tf_op jit(solution)/shard_map/tji,tjf->tif/dot_general | solution.py:41
  356.7 23.5 %copy.15 = f32[352,128,128]{2,1,0:T(8,128)} copy(f32[352,128,128]{1,2,0:T(8,128)} %fusion.7) | data formatting | bytes 46137344 | tf_op jit(solution)/shard_map/tji,tjf->tif/dot_general | solution.py:41
  380.4 46.0 %scatter_fusion.1 = f32[33,128,128]{2,1,0:T(8,128)S(1)} fusion(f32[33,128,128]{2,1,0:T(8,128)S(1)} %broadcast.191, s32[352]{0:T(512)S(1)} %get-tuple-element.11, f32[352,128,128]{2,1,0:T(8,128)} %copy.15), kind=kCustom, calls=%fused_computation.3 | custom fusion | flops 5767168 | bytes 69207424 | tf_op jit(solution)/shard_map/scatter-add | solution.py:45
  426.4 1.5 slice.13
  428.0 1.6 multiply_convert_fusion.1
  429.6 92.6 %reduce-scatter.2.cloned.1.call-done = f32[256,128]{1,0:T(8,128)} async-done(((f32[4096,128]{1,0:T(8,128)}), f32[256,128]{1,0:T(8,128)}) %reduce-scatter.2.cloned.1.call-update) | async-done | bytes 131088 | tf_op jit(solution)/shard_map/reduce_scatter | solution.py:48
  522.2 1.7 convolution_bitcast_fusion
  524.0 1.7 convolution_convert_fusion
  525.7 237.9 %all-reduce.5.cloned.1.call-done = f32[128,128]{0,1:T(8,128)} async-done(((f32[128,128]{0,1:T(8,128)}), f32[128,128]{0,1:T(8,128)}) %all-reduce.5.cloned.1.call-update) | async-done | bytes 65552 | tf_op jit(solution)/shard_map/psum | solution.py:56
  763.5 0.8 broadcast_multiply_fusion
  764.4 0.7 copy.16
  (18 shorter events, 1.7 us)
Async XLA Ops:
  7.2 0.8 copy-start
  7.2 64.1 %all-gather.3.cloned.1.call-start = ((), (), s32[]{:S(2)}) async-start(), calls=%async_computation.1 | async-start | bytes 1114112 | tf_op jit(solution)/shard_map/all_gather | solution.py:27
  9.6 166.1 %all-gather.5.cloned.1.call-start = ((), (), s32[]{:S(2)}) async-start(), calls=%async_computation.3 | async-start | bytes 1114112 | tf_op jit(solution)/shard_map/all_gather | solution.py:38
  10.3 318.3 %all-reduce.3.cloned.1.call-start = ((), (), s32[]{:S(2)}) async-start(), calls=%async_computation.2 | async-start | bytes 4194304 | tf_op jit(solution)/shard_map/psum | solution.py:35
  175.4 346.8 %reduce-scatter.2.cloned.1.call-start = ((), (), s32[]{:S(2)}) async-start(), calls=%async_computation.4 | async-start | bytes 2228224 | tf_op jit(solution)/shard_map/reduce_scatter | solution.py:48
  380.4 143.5 %copy-start.1 = (bf16[128,128]{1,0:T(8,128)(2,1)S(1)}, bf16[128,128]{1,0:T(8,128)(2,1)}, u32[]{:S(2)}) copy-start(bf16[128,128]{1,0:T(8,128)(2,1)} %param.7) | copy-start | bytes 98308
  428.0 335.5 %all-reduce.5.cloned.1.call-start = ((), (), s32[]{:S(2)}) async-start(), calls=%async_computation.5 | async-start | bytes 131072 | tf_op jit(solution)/shard_map/psum | solution.py:56
Sparse Core Ops, SparseCore 0:
  11.3 59.9 all-gather.2
  73.1 65.9 all-gather.4
  175.5 153.0 all-reduce.2
  428.1 94.0 reduce-scatter.1
  528.1 235.3 all-reduce.4
where the time goes:
time: 774 us; the launch traced here: 772 us
  waiting for transfers between devices  543 us (70%)
  other arithmetic  98.5 us (13%)
  local copies, waits for them, and re-layouts  75.1 us (10%)
  matrix products  40 us (5%)
  between operations  14.5 us (2%)
    psum x1, waiting for transfers between devices, body(): weight_grad = lax.psum(weight_term, ('row', 'col')) / math.sqrt(node_total)  238 us
    psum x1, waiting for transfers between devices, body(): summed = lax.psum(partial_value, 'col')  153 us
    reduce_scatter x1, waiting for transfers between devices, body(): lax.psum_scatter(back_partial, 'row', scatter_dimension=0, tiled=True)  92.6 us
    all_gather x1, waiting for transfers between devices, body(): proj_block = lax.all_gather(projected, 'row', axis=0, tiled=True)  58.8 us
    scatter-add x1, other arithmetic, body(): jax.ops.segment_sum(products, fwd_targets, tile_rows + 1)[:tile_rows]  46 us
    scatter-add x1, other arithmetic, body(): jax.ops.segment_sum(back_products, back_targets, tile_cols + 1)[:tile_cols]  46 us
    dot_general x1, local copies, waits for them, and re-layouts, body(): jnp.einsum('tij,tjf->tif', tile_vals, gathered, preferred_element_type=jn...  23.5 us
    dot_general x1, local copies, waits for them, and re-layouts, body(): jnp.einsum('tji,tjf->tif', tile_vals, grad_tiles, preferred_element_type=...  23.5 us
  transfers between devices with their start and end apart: 5, of which 4 were waited for; matrix products, arithmetic and copies ran while one was open for 14% of the time, Pallas kernels for 0%

commit v1 on v0

--- a/solution.py
+++ b/solution.py
@@ -53,7 +53,7 @@
     )
     weight_term = jnp.dot(features.T, grad_proj, preferred_element_type=jnp.float32)
     node_total = share_rows * row_count * col_count
-    weight_grad = lax.psum(weight_term, ("row", "col")) / math.sqrt(node_total)
+    weight_grad = lax.psum(lax.psum(weight_term, "col"), "row") / math.sqrt(node_total)
     return (hidden, feature_grad, weight_grad)
 
 

time: 774 us -> 847 us (1.094)
  waiting for transfers between devices: 543 us -> 614 us
    psum x1 -> x2, waiting for transfers between devices: 238 us -> 308 us  [the longest x1 171 us: body(): lax.psum(lax.psum(weight_term, 'col'), 'row') / math.sqrt(node_total)]
  transfers between devices with their start and end apart: 5 -> 6, of which waited for: 4 -> 5; matrix products, arithmetic and copies ran while one was open for 14% -> 13% of each run, Pallas kernels for 0% -> 0%
where the time goes in v1:
time: 847 us; the launch traced here: 843 us
  waiting for transfers between devices  614 us (72%)
  other arithmetic  98.5 us (12%)
  local copies, waits for them, and re-layouts  75.1 us (9%)
  matrix products  40 us (5%)
  between operations  14.8 us (2%)
    psum x1, waiting for transfers between devices, body(): lax.psum(lax.psum(weight_term, 'col'), 'row') / math.sqrt(node_total)  171 us
    psum x1, waiting for transfers between devices, body(): summed = lax.psum(partial_value, 'col')  153 us
    psum x1, waiting for transfers between devices, body(): lax.psum(weight_term, 'col')  136 us
    reduce_scatter x1, waiting for transfers between devices, body(): lax.psum_scatter(back_partial, 'row', scatter_dimension=0, tiled=True)  94.2 us
    all_gather x1, waiting for transfers between devices, body(): proj_block = lax.all_gather(projected, 'row', axis=0, tiled=True)  58.8 us
    scatter-add x1, other arithmetic, body(): jax.ops.segment_sum(products, fwd_targets, tile_rows + 1)[:tile_rows]  46 us
    scatter-add x1, other arithmetic, body(): jax.ops.segment_sum(back_products, back_targets, tile_cols + 1)[:tile_cols]  46 us
    dot_general x1, local copies, waits for them, and re-layouts, body(): jnp.einsum('tij,tjf->tif', tile_vals, gathered, preferred_element_type=jn...  23.5 us
  transfers between devices with their start and end apart: 6, of which 5 were waited for; matrix products, arithmetic and copies ran while one was open for 13% of the time, Pallas kernels for 0%

profile of v1, /device:TPU:1, one launch (start us, length us, event | category | flops | bytes accessed | tf_op | source)
XLA Modules:
  0.0 843.4 jit_solution(18120193965231730082)
XLA Ops:
  7.2 0.8 copy-done
  8.0 1.5 convolution_convert_fusion.1
  11.7 0.7 fusion.13
  12.4 58.8 %all-gather.3.cloned.1.call-done = bf16[4096,128]{1,0:T(8,128)(2,1)} async-done(((bf16[256,128]{1,0:T(8,128)(2,1)}), bf16[4096,128]{1,0:T(8,128)(2,1)}) %all-gather.3.cloned.1.call-update) | async-done | bytes 1048592 | tf_op jit(solution)/shard_map/all_gather | solution.py:27
  71.3 12.2 %gather_fusion = bf16[352,128,128]{2,1,0:T(8,128)(2,1)} fusion(bf16[32,128,128]{2,1,0:T(8,128)(2,1)} %bitcast.41, s32[1024]{0:T(1024)S(1)} %pad_clamp_fusion.1), kind=kCustom, calls=%fused_computation | custom fusion | bytes 23070080 | tf_op jit(solution)/shard_map/gather | solution.py:29
  83.5 20.6 %fusion.4 = f32[352,128,128]{1,2,0:T(8,128)} fusion(bf16[352,128,128]{2,1,0:T(8,128)(2,1)} %gather_fusion, bf16[1,1,352,128,128]{4,3,2,1,0:T(8,128)(2,1)} %param.8), kind=kOutput, calls=%fused_computation.8 | convolution fusion | flops 1476395008 | bytes 46137344 | tf_op jit(solution)/shard_map/tij,tjf->tif/dot_general | solution.py:30
  104.1 23.5 %copy.13 = f32[352,128,128]{2,1,0:T(8,128)} copy(f32[352,128,128]{1,2,0:T(8,128)} %fusion.4) | data formatting | bytes 46137344 | tf_op jit(solution)/shard_map/tij,tjf->tif/dot_general | solution.py:30
  127.8 46.0 %scatter_fusion = f32[33,128,128]{2,1,0:T(8,128)S(1)} fusion(f32[33,128,128]{2,1,0:T(8,128)S(1)} %broadcast.191.clone, s32[352]{0:T(512)S(1)} %get-tuple-element.10, f32[352,128,128]{2,1,0:T(8,128)} %copy.13), kind=kCustom, calls=%fused_computation.2 | custom fusion | flops 5767168 | bytes 69207424 | tf_op jit(solution)/shard_map/scatter-add | solution.py:32
  173.9 1.5 slice.12
  175.7 153.0 %all-reduce.4.cloned.1.call-done = f32[4096,128]{1,0:T(8,128)} async-done(((f32[4096,128]{1,0:T(8,128)}), f32[4096,128]{1,0:T(8,128)}) %all-reduce.4.cloned.1.call-update) | async-done | bytes 2097168 | tf_op jit(solution)/shard_map/psum | solution.py:35
  328.6 2.6 multiply_convert_fusion
  331.3 11.0 %gather_fusion.1 = bf16[352,128,128]{2,1,0:T(8,128)(2,1)} fusion(bf16[32,128,128]{2,1,0:T(8,128)(2,1)S(1)} %bitcast.40, s32[1024]{0:T(1024)S(1)} %pad_clamp_fusion), kind=kCustom, calls=%fused_computation.1 | custom fusion | bytes 23070080 | tf_op jit(solution)/shard_map/gather | solution.py:40
  342.3 14.4 %fusion.7 = f32[352,128,128]{1,2,0:T(8,128)} fusion(bf16[352,128,128]{2,1,0:T(8,128)(2,1)} %gather_fusion.1, bf16[1,1,352,128,128]{4,3,2,1,0:T(8,128)(2,1)} %param.8), kind=kOutput, calls=%fused_computation.9 | convolution fusion | flops 1476395008 | bytes 46137344 | tf_op jit(solution)/shard_map/tji,tjf->tif/dot_general | solution.py:41
  356.7 23.5 %copy.15 = f32[352,128,128]{2,1,0:T(8,128)} copy(f32[352,128,128]{1,2,0:T(8,128)} %fusion.7) | data formatting | bytes 46137344 | tf_op jit(solution)/shard_map/tji,tjf->tif/dot_general | solution.py:41
  380.4 46.0 %scatter_fusion.1 = f32[33,128,128]{2,1,0:T(8,128)S(1)} fusion(f32[33,128,128]{2,1,0:T(8,128)S(1)} %broadcast.191, s32[352]{0:T(512)S(1)} %get-tuple-element.11, f32[352,128,128]{2,1,0:T(8,128)} %copy.15), kind=kCustom, calls=%fused_computation.3 | custom fusion | flops 5767168 | bytes 69207424 | tf_op jit(solution)/shard_map/scatter-add | solution.py:45
  426.4 1.5 slice.13
  428.0 94.2 %reduce-scatter.2.cloned.1.call-done = f32[256,128]{1,0:T(8,128)} async-done(((f32[4096,128]{1,0:T(8,128)}), f32[256,128]{1,0:T(8,128)}) %reduce-scatter.2.cloned.1.call-update) | async-done | bytes 131088 | tf_op jit(solution)/shard_map/reduce_scatter | solution.py:48
  522.2 1.7 convolution_bitcast_fusion
  524.0 1.6 multiply_convert_fusion.1
  525.6 136.4 %all-reduce.6.cloned.1.call-done = f32[128,128]{0,1:T(8,128)} async-done(((f32[128,128]{0,1:T(8,128)}), f32[128,128]{0,1:T(8,128)}) %all-reduce.6.cloned.1.call-update) | async-done | bytes 65552 | tf_op jit(solution)/shard_map/psum | solution.py:56
  662.0 1.7 convolution_convert_fusion
  663.7 171.3 %all-reduce.8.cloned.1.call-done = f32[128,128]{0,1:T(8,128)} async-done(((f32[128,128]{0,1:T(8,128)}), f32[128,128]{0,1:T(8,128)}) %all-reduce.8.cloned.1.call-update) | async-done | bytes 65552 | tf_op jit(solution)/shard_map/psum | solution.py:56
  835.0 0.8 broadcast_multiply_fusion
  835.8 0.7 copy.16
  (21 shorter events, 2.4 us)
Async XLA Ops:
  7.2 0.8 copy-start
  7.2 64.1 %all-gather.3.cloned.1.call-start = ((), (), s32[]{:S(2)}) async-start(), calls=%async_computation.1 | async-start | bytes 1114112 | tf_op jit(solution)/shard_map/all_gather | solution.py:27
  9.6 166.1 %all-gather.5.cloned.1.call-start = ((), (), s32[]{:S(2)}) async-start(), calls=%async_computation.3 | async-start | bytes 1114112 | tf_op jit(solution)/shard_map/all_gather | solution.py:38
  10.3 318.3 %all-reduce.4.cloned.1.call-start = ((), (), s32[]{:S(2)}) async-start(), calls=%async_computation.2 | async-start | bytes 4194304 | tf_op jit(solution)/shard_map/psum | solution.py:35
  175.4 346.8 %reduce-scatter.2.cloned.1.call-start = ((), (), s32[]{:S(2)}) async-start(), calls=%async_computation.4 | async-start | bytes 2228224 | tf_op jit(solution)/shard_map/reduce_scatter | solution.py:48
  380.4 281.6 %copy-start.1 = (bf16[128,128]{1,0:T(8,128)(2,1)S(1)}, bf16[128,128]{1,0:T(8,128)(2,1)}, u32[]{:S(2)}) copy-start(bf16[128,128]{1,0:T(8,128)(2,1)} %param.7) | copy-start | bytes 98308
  428.0 234.0 %all-reduce.6.cloned.1.call-start = ((), (), s32[]{:S(2)}) async-start(), calls=%async_computation.5 | async-start | bytes 131072 | tf_op jit(solution)/shard_map/psum | solution.py:56
  523.9 311.0 %all-reduce.8.cloned.1.call-start = ((), (), s32[]{:S(2)}) async-start(), calls=%async_computation.6 | async-start | bytes 131072 | tf_op jit(solution)/shard_map/psum | solution.py:56
Sparse Core Ops, SparseCore 0:
  11.3 59.9 all-gather.2
  73.1 65.9 all-gather.4
  175.5 153.0 all-reduce.3
  428.1 94.0 reduce-scatter.1
  525.2 136.6 all-reduce.5
  664.6 170.3 all-reduce.7
